TPU v7x, 512 devices: a whole 4x4x16 slice. The times are simulated.
512 devices in a mesh: dp: 32 (over z, core), member: 16 (over y, x).
Axes of the slice: x: 4, y: 4, z: 16, core: 2. Of those that a mesh axis runs over, the one named last changes fastest.
Arguments:
- tokens: bfloat16 [4096, 4096], P('dp', 'member'), may hold values from -6 to 6
- routes: int32 [4096, 2], P('dp'), may hold values from 0 to 7, all different within a row; in each aligned block of 128 rows (0 to 127, 128 to 255, ...) at most 34 rows name the same one
- route_weights: float32 [4096, 2], P('dp'), may hold values from 0.2 to 1
- up_stacked: bfloat16 [8, 4096, 7168], P(None, ('member', 'dp')), may hold values from -0.09375 to 0.09375
- down_stacked: bfloat16 [8, 4096, 7168], P(None, ('member', 'dp')), may hold values from -0.0625 to 0.0625
- cotangent: bfloat16 [4096, 4096], P('dp', 'member'), may hold values from -6 to 6
Outputs:
- mixed: bfloat16 [4096, 4096], P('dp', 'member')
- grad_tokens: bfloat16 [4096, 4096], P('dp', 'member')
- grad_up: bfloat16 [32, 4096, 1792], P('dp', 'member')
- grad_down: bfloat16 [32, 4096, 1792], P('dp', 'member')
Inputs may be any that keep to these rules, and one draw needn't show every extreme that they name: `routes`: each row names two different experts. In each aligned block of 128 rows no expert is named by more than 34 rows, and in some block some expert is named by exactly 34 rows.
All inputs are finite; a program needn't handle non-finite values.
Results may differ from a plain program's by a relative error of at most 0.018.
Values may be sent and summed in bfloat16 or wider, within the bound.
A program may use at most 64 MiB of HBM per device.

v0:
```python
import jax
import jax.numpy as jnp
from jax import lax
from jax.sharding import PartitionSpec as P

FF_W = 7168
E = 8
CAP = 34


def contract(left, right, left_dim, right_dim):
    return lax.dot_general(
        left, right, (((left_dim,), (right_dim,)), ((), ())), preferred_element_type=jnp.float32
    )


def body(tokens, routes, route_weights, up_stacked, down_stacked, cotangent):
    dp_count = lax.axis_size("dp")
    member_count = lax.axis_size("member")
    quarters = dp_count // E
    share_rows = up_stacked.shape[1]
    features = tokens.shape[1]
    hidden_own = FF_W // quarters
    per_member = hidden_own // member_count
    slots_all = E * CAP
    up_parts = (
        up_stacked.reshape(E, share_rows, quarters, hidden_own)
        .transpose(0, 2, 1, 3)
        .reshape(dp_count, share_rows, hidden_own)
    )
    down_parts = (
        down_stacked.reshape(E, share_rows, quarters, hidden_own)
        .transpose(0, 2, 1, 3)
        .reshape(dp_count, share_rows, hidden_own)
    )
    up_own, down_own = (
        lax.all_to_all(up_parts, "dp", split_axis=0, concat_axis=1, tiled=True),
        lax.all_to_all(down_parts, "dp", split_axis=0, concat_axis=1, tiled=True),
    )
    up_own = up_own.reshape(dp_count * share_rows, hidden_own)
    down_own = down_own.reshape(dp_count * share_rows, hidden_own)
    chosen = (routes[:, :, None] == jnp.arange(E, dtype=jnp.int32)[None, None, :]).astype(jnp.int32)
    flat_hits = chosen.reshape(-1, E)
    before = jnp.cumsum(flat_hits, axis=0) - flat_hits
    slot_pos = jnp.sum(before * flat_hits, axis=1).reshape(-1, 2)
    target = routes * CAP + slot_pos
    slot_hits = jnp.arange(slots_all, dtype=jnp.int32)[:, None, None] == target[None, :, :]
    pick_table = jnp.sum(slot_hits.astype(jnp.float32), axis=2)
    weighted = jnp.sum(jnp.where(slot_hits, route_weights[None, :, :], 0.0), axis=2)
    x_local = jnp.dot(
        pick_table.astype(jnp.bfloat16), tokens, preferred_element_type=jnp.float32
    ).astype(jnp.bfloat16)
    d_local = jnp.dot(
        weighted, cotangent.astype(jnp.float32), precision=lax.Precision.HIGHEST
    ).astype(jnp.bfloat16)

    def spread(local):
        return jnp.broadcast_to(
            local.reshape(E, 1, CAP, features), (E, quarters, CAP, features)
        ).reshape(dp_count, CAP, features)

    def collect(returned):
        return jnp.sum(returned.reshape(E, quarters, CAP, features), axis=1).reshape(
            slots_all, features
        )

    x_in = lax.all_to_all(spread(x_local), "dp", split_axis=0, concat_axis=0, tiled=True).reshape(
        dp_count * CAP, features
    )
    partial_value = jnp.dot(x_in, up_own, preferred_element_type=jnp.float32).astype(jnp.bfloat16)
    pre_full = lax.psum(partial_value, "member").astype(jnp.float32)
    act_full = jax.nn.silu(pre_full).astype(jnp.bfloat16)
    y_part = contract(act_full, down_own, 1, 1)
    y_part, pre_full, act_full = (y_part, pre_full, act_full)
    y_back = lax.all_to_all(
        y_part.reshape(dp_count, CAP, features).astype(jnp.bfloat16),
        "dp",
        split_axis=0,
        concat_axis=0,
        tiled=True,
    ).astype(jnp.float32)
    d_in = lax.all_to_all(spread(d_local), "dp", split_axis=0, concat_axis=0, tiled=True).reshape(
        dp_count * CAP, features
    )
    d_act = lax.psum_scatter(
        contract(down_own, d_in, 0, 1).astype(jnp.bfloat16),
        "member",
        scatter_dimension=0,
        tiled=True,
    ).astype(jnp.float32)
    own_start = lax.axis_index("member") * per_member
    pre_share = lax.dynamic_slice_in_dim(pre_full, own_start, per_member, 1).T
    sigma = jax.nn.sigmoid(pre_share)
    d_share = (d_act * sigma * (1.0 + pre_share * (1.0 - sigma))).astype(jnp.bfloat16)
    d_pre = lax.all_gather(d_share, "member", axis=0, tiled=True)
    g_down = contract(d_in, act_full, 0, 0)
    g_up = contract(x_in, d_pre, 0, 1)
    dx_part = contract(d_pre, up_own, 0, 1)
    dx_part, g_up, g_down = (dx_part, g_up, g_down)
    dx_back = lax.all_to_all(
        dx_part.reshape(dp_count, CAP, features).astype(jnp.bfloat16),
        "dp",
        split_axis=0,
        concat_axis=0,
        tiled=True,
    ).astype(jnp.float32)
    y_slots = collect(y_back)
    dx_slots = collect(dx_back)
    mixed = jnp.dot(weighted.T, y_slots, precision=lax.Precision.HIGHEST).astype(jnp.bfloat16)
    grad_tokens = jnp.dot(pick_table.T, dx_slots, precision=lax.Precision.HIGHEST).astype(
        jnp.bfloat16
    )
    grad_up = g_up.astype(jnp.bfloat16).reshape(1, features, hidden_own)
    grad_down = g_down.astype(jnp.bfloat16).reshape(1, features, hidden_own)
    return (mixed, grad_tokens, grad_up, grad_down)


def solution(mesh):
    placed = (
        P("dp", "member"),
        P("dp", None),
        P("dp", None),
        P(None, ("member", "dp"), None),
        P(None, ("member", "dp"), None),
        P("dp", "member"),
    )
    return jax.shard_map(
        body,
        mesh=mesh,
        in_specs=placed,
        out_specs=(
            P("dp", "member"),
            P("dp", "member"),
            P("dp", "member", None),
            P("dp", "member", None),
        ),
        check_vma=False,
    )
```

profile of v0, /device:TPU:1, one launch (start us, length us, event | category | flops | bytes accessed | tf_op | source)
XLA Modules:
  0.0 533.8 jit_solution(7201500621114122409)
XLA Ops:
  7.2 0.0 copy-start
  7.2 0.8 copy.35
  8.0 0.1 eq.44
  8.1 0.1 eq.40
  8.3 0.6 reduce-window.6
  8.9 0.2 slice_reduce_fusion
  9.1 0.1 fusion.14
  9.2 0.1 reshape.98
  9.4 0.1 copy.37
  9.4 0.7 multiply_add_fusion
  10.1 0.8 convert_reduce_fusion.2
  10.9 0.0 copy-done
  10.9 0.3 convolution_convert_fusion.6
  11.2 0.9 broadcast_in_dim.36
  12.1 16.8 %all-to-all-start.4 = ((bf16[32,34,256]{2,1,0:T(8,128)(2,1)}), bf16[32,34,256]{2,1,0:T(8,128)(2,1)S(1)}, u32[]{:S(2)}, u32[]{:S(2)}) async-start(bf16[32,34,256]{2,1,0:T(8,128)(2,1)} %bitcast.9), calls=%async_computation.4 | async-start | bytes 1310720 | tf_op jit(solution)/shard_map/all_to_all | solution.py:82
  28.9 1.0 convolution_convert_fusion.7
  30.0 38.0 %all-to-all-done.4 = bf16[32,34,256]{2,1,0:T(8,128)(2,1)S(1)} async-done(((bf16[32,34,256]{2,1,0:T(8,128)(2,1)}), bf16[32,34,256]{2,1,0:T(8,128)(2,1)S(1)}, u32[]{:S(2)}, u32[]{:S(2)}) %all-to-all-start.4) | async-done | bytes 557088 | tf_op jit(solution)/shard_map/all_to_all | solution.py:82
  68.0 0.9 broadcast_in_dim.34
  68.8 4.1 all-to-all-start
  72.9 1.3 fusion.16
  74.3 1.0 pad_maximum_fusion.1
  75.3 36.7 %all-to-all-done = bf16[32,34,256]{2,1,0:T(8,128)(2,1)S(1)} async-done(((bf16[32,34,256]{2,1,0:T(8,128)(2,1)}), bf16[32,34,256]{2,1,0:T(8,128)(2,1)S(1)}, u32[]{:S(2)}, u32[]{:S(2)}) %all-to-all-start) | async-done | bytes 557088 | tf_op jit(solution)/shard_map/all_to_all | solution.py:67
  112.0 0.0 copy-start.2
  112.0 0.8 copy-done.2
  112.8 4.5 all-to-all-start.2
  117.3 1.3 fusion.17
  118.7 1.0 pad_maximum_fusion
  119.7 47.9 %all-to-all-done.2 = bf16[32,8,1792]{2,1,0:T(8,128)(2,1)S(1)} async-done(((bf16[32,8,1792]{2,1,0:T(8,128)(2,1)}), bf16[32,8,1792]{2,1,0:T(8,128)(2,1)S(1)}, u32[]{:S(2)}, u32[]{:S(2)}) %all-to-all-start.2) | async-done | bytes 917536 | tf_op jit(solution)/shard_map/all_to_all | solution.py:38
  167.6 4.5 all-to-all-start.1
  172.1 0.0 all-reduce.4.cloned.1.call-start
  172.2 1.0 reshape.109
  173.1 1.3 reshape.100
  174.4 4.4 convolution_convert_fusion
  178.8 6.4 %copy.38 = bf16[1792,1088]{0,1:T(8,128)(2,1)} copy(bf16[1792,1088]{1,0:T(8,128)(2,1)} %convolution_convert_fusion) | data formatting | bytes 7798784 | tf_op jit(solution)/shard_map/convert_element_type | solution.py:86
  185.2 37.2 %all-to-all-done.1 = bf16[32,8,1792]{2,1,0:T(8,128)(2,1)S(1)} async-done(((bf16[32,8,1792]{2,1,0:T(8,128)(2,1)}), bf16[32,8,1792]{2,1,0:T(8,128)(2,1)S(1)}, u32[]{:S(2)}, u32[]{:S(2)}) %all-to-all-start.1) | async-done | bytes 917536 | tf_op jit(solution)/shard_map/all_to_all | solution.py:37
  222.4 3.1 convolution_convert_fusion.1
  225.5 0.0 all-reduce.4.cloned.1.call-update
  225.5 0.0 all-gather.2.cloned.1.call-start
  225.6 1.3 dynamic-slice
  227.5 156.5 %all-reduce.4.cloned.1.call-done = (bf16[1088,1792]{1,0:T(8,128)(2,1)}, bf16[1792,1088]{0,1:T(8,128)(2,1)}) async-done(((bf16[1088,1792]{1,0:T(8,128)(2,1)}, bf16[1792,1088]{0,1:T(8,128)(2,1)}), (bf16[1088,1792]{1,0:T(8,128)(2,1)}, bf16[1792,1088]{0,1:T(8,128)(2,1)})) %all-reduce.4.cloned.1.call-update) | async-done | bytes 7798800 | tf_op jit(solution)/shard_map/psum | solution.py:71
  384.0 2.7 convert_element_type.65
  386.7 1.4 fusion.11
  388.1 0.9 copy.39
  389.0 0.0 all-gather.2.cloned.1.call-update
  389.0 5.0 multiply_convert_fusion
  394.0 6.9 %dot_general.38 = bf16[32,34,1792]{2,1,0:T(8,128)(2,1)} reshape(bf16[1088,1792]{1,0:T(8,128)(2,1)} %multiply_convert_fusion) | data formatting | bytes 7798784 | tf_op jit(solution)/shard_map/dot_general | solution.py:12
  400.9 4.6 convolution_convert_fusion.5
  405.5 13.0 %all-to-all-start.3 = ((bf16[32,34,256]{2,1,0:T(8,128)(2,1)}), bf16[32,34,256]{2,1,0:T(8,128)(2,1)S(1)}, u32[]{:S(2)}, u32[]{:S(2)}) async-start(bf16[32,34,256]{2,1,0:T(8,128)(2,1)} %convolution_convert_fusion.5), calls=%async_computation.3 | async-start | bytes 1310720 | tf_op jit(solution)/shard_map/all_to_all | solution.py:75
  418.5 37.1 %all-gather.2.cloned.1.call-done = bf16[1792,1088]{1,0:T(8,128)(2,1)} async-done(((bf16[112,1088]{1,0:T(8,128)(2,1)}), bf16[1792,1088]{1,0:T(8,128)(2,1)}) %all-gather.2.cloned.1.call-update) | async-done | bytes 3899408 | tf_op jit(solution)/shard_map/all_gather | solution.py:95
  455.6 6.4 %copy.40 = bf16[1088,1792]{1,0:T(8,128)(2,1)} copy(bf16[1088,1792]{0,1:T(8,128)(2,1)} %bitcast.72) | data formatting | bytes 7798784 | tf_op jit(solution)/shard_map/dot_general | solution.py:12
  462.0 6.9 %dot_general.44 = bf16[32,34,1792]{2,1,0:T(8,128)(2,1)} reshape(bf16[1088,1792]{1,0:T(8,128)(2,1)} %copy.40) | data formatting | bytes 7798784 | tf_op jit(solution)/shard_map/dot_general | solution.py:12
  468.9 4.7 convolution_convert_fusion.4
  473.6 0.0 all-to-all-done.3
  473.6 13.0 %all-to-all-start.5 = ((bf16[32,34,256]{2,1,0:T(8,128)(2,1)}), bf16[32,34,256]{2,1,0:T(8,128)(2,1)S(1)}, u32[]{:S(2)}, u32[]{:S(2)}) async-start(bf16[32,34,256]{2,1,0:T(8,128)(2,1)} %convolution_convert_fusion.4), calls=%async_computation.5 | async-start | bytes 1310720 | tf_op jit(solution)/shard_map/all_to_all | solution.py:100
  486.6 0.0 copy-done.3
  486.6 4.4 fusion.1
  491.0 0.1 convert_reduce_fusion.1
  491.2 0.0 copy-start.1
  491.2 1.1 convolution_convert_fusion.9
  492.3 4.5 fusion
  496.8 28.9 %all-to-all-done.5 = bf16[32,34,256]{2,1,0:T(8,128)(2,1)S(1)} async-done(((bf16[32,34,256]{2,1,0:T(8,128)(2,1)}), bf16[32,34,256]{2,1,0:T(8,128)(2,1)S(1)}, u32[]{:S(2)}, u32[]{:S(2)}) %all-to-all-start.5) | async-done | bytes 557088 | tf_op jit(solution)/shard_map/all_to_all | solution.py:100
  525.7 0.1 convert_reduce_fusion
  525.8 1.1 convolution_convert_fusion.8
  527.0 0.0 copy-done.1
  (8 shorter events, 0.2 us)
Async XLA Ops:
  7.2 3.7 copy-start
  12.1 55.9 %all-to-all-start.4 = ((bf16[32,34,256]{2,1,0:T(8,128)(2,1)}), bf16[32,34,256]{2,1,0:T(8,128)(2,1)S(1)}, u32[]{:S(2)}, u32[]{:S(2)}) async-start(bf16[32,34,256]{2,1,0:T(8,128)(2,1)} %bitcast.9), calls=%async_computation.4 | async-start | bytes 1310720 | tf_op jit(solution)/shard_map/all_to_all | solution.py:82
  68.8 43.1 %all-to-all-start = ((bf16[32,34,256]{2,1,0:T(8,128)(2,1)}), bf16[32,34,256]{2,1,0:T(8,128)(2,1)S(1)}, u32[]{:S(2)}, u32[]{:S(2)}) async-start(bf16[32,34,256]{2,1,0:T(8,128)(2,1)} %bitcast.2), calls=%async_computation | async-start | bytes 1310720 | tf_op jit(solution)/shard_map/all_to_all | solution.py:67
  112.0 0.8 copy-start.2
  112.8 54.7 %all-to-all-start.2 = ((bf16[32,8,1792]{2,1,0:T(8,128)(2,1)}), bf16[32,8,1792]{2,1,0:T(8,128)(2,1)S(1)}, u32[]{:S(2)}, u32[]{:S(2)}) async-start(bf16[32,8,1792]{2,1,0:T(8,128)(2,1)} %bitcast.5), calls=%async_computation.2 | async-start | bytes 1835008 | tf_op jit(solution)/shard_map/all_to_all | solution.py:38
  167.6 54.8 %all-to-all-start.1 = ((bf16[32,8,1792]{2,1,0:T(8,128)(2,1)}), bf16[32,8,1792]{2,1,0:T(8,128)(2,1)S(1)}, u32[]{:S(2)}, u32[]{:S(2)}) async-start(bf16[32,8,1792]{2,1,0:T(8,128)(2,1)} %bitcast.3), calls=%async_computation.1 | async-start | bytes 1835008 | tf_op jit(solution)/shard_map/all_to_all | solution.py:37
  172.1 211.8 %all-reduce.4.cloned.1.call-start = ((), (), s32[]{:S(2)}) async-start(), calls=%async_computation.7 | async-start | bytes 15597568 | tf_op jit(solution)/shard_map/psum | solution.py:71
  225.5 230.1 %all-gather.2.cloned.1.call-start = ((), (), s32[]{:S(2)}) async-start(), calls=%async_computation.6 | async-start | bytes 4386816 | tf_op jit(solution)/shard_map/all_gather | solution.py:95
  405.5 68.1 %all-to-all-start.3 = ((bf16[32,34,256]{2,1,0:T(8,128)(2,1)}), bf16[32,34,256]{2,1,0:T(8,128)(2,1)S(1)}, u32[]{:S(2)}, u32[]{:S(2)}) async-start(bf16[32,34,256]{2,1,0:T(8,128)(2,1)} %convolution_convert_fusion.5), calls=%async_computation.3 | async-start | bytes 1310720 | tf_op jit(solution)/shard_map/all_to_all | solution.py:75
  468.9 17.7 %copy-start.3 = (bf16[1088,256]{1,0:T(8,128)(2,1)S(1)}, bf16[1088,256]{1,0:T(8,128)(2,1)}, u32[]{:S(2)}) copy-start(bf16[1088,256]{1,0:T(8,128)(2,1)} %reshape.109) | copy-start | bytes 1671172
  473.6 52.1 %all-to-all-start.5 = ((bf16[32,34,256]{2,1,0:T(8,128)(2,1)}), bf16[32,34,256]{2,1,0:T(8,128)(2,1)S(1)}, u32[]{:S(2)}, u32[]{:S(2)}) async-start(bf16[32,34,256]{2,1,0:T(8,128)(2,1)} %convolution_convert_fusion.4), calls=%async_computation.5 | async-start | bytes 1310720 | tf_op jit(solution)/shard_map/all_to_all | solution.py:100
  491.2 35.8 %copy-start.1 = (bf16[128,256]{1,0:T(8,128)(2,1)S(1)}, bf16[128,256]{1,0:T(8,128)(2,1)}, u32[]{:S(2)}) copy-start(bf16[128,256]{1,0:T(8,128)(2,1)} %param.11) | copy-start | bytes 196612
Sparse Core Ops, SparseCore 0:
  225.7 158.2 all-reduce.3
  389.1 66.4 all-gather.1
where the time goes:
time: 535 us; the launch traced here: 534 us
  waiting for transfers between devices  382 us (71%)
  starting transfers between devices  55.9 us (10%)
  local copies, waits for them, and re-layouts  38 us (7%)
  matrix products  29.2 us (5%)
  between operations  14.9 us (3%)
  other arithmetic  13.5 us (3%)
    psum x1, waiting for transfers between devices, body(): pre_full = lax.psum(partial_value, 'member').astype(jnp.float32)  156 us
    all_to_all x1, waiting for transfers between devices, body(): lax.all_to_all(down_parts, 'dp', split_axis=0, concat_axis=1, tiled=True)  47.9 us
    all_to_all x1, waiting for transfers between devices, body(): lax.all_to_all(spread(d_local), 'dp', split_axis=0, concat_axis=0, tiled=...  38 us
    all_to_all x1, waiting for transfers between devices, body(): lax.all_to_all(up_parts, 'dp', split_axis=0, concat_axis=1, tiled=True)  37.2 us
    all_gather x1, waiting for transfers between devices, body(): d_pre = lax.all_gather(d_share, 'member', axis=0, tiled=True)  37.1 us
    all_to_all x1, waiting for transfers between devices, body(): lax.all_to_all(spread(x_local), 'dp', split_axis=0, concat_axis=0, tiled=...  36.7 us
    all_to_all x1, waiting for transfers between devices, body(): lax.all_to_all(dx_part.reshape(dp_count, CAP, features).astype(jnp.bfloat...  28.9 us
    dot_general x5, matrix products, contract(): lax.dot_general(left, right, (((left_dim,), (right_dim,)), ((), ())), pre...  22.5 us
  transfers between devices with their start and end apart: 8, of which 7 were waited for; matrix products, arithmetic and copies ran while one was open for 12% of the time, Pallas kernels for 0%

commit v1 on v0

--- a/solution.py
+++ b/solution.py
@@ -92,7 +92,8 @@
     pre_share = lax.dynamic_slice_in_dim(pre_full, own_start, per_member, 1).T
     sigma = jax.nn.sigmoid(pre_share)
     d_share = (d_act * sigma * (1.0 + pre_share * (1.0 - sigma))).astype(jnp.bfloat16)
-    d_pre = lax.all_gather(d_share, "member", axis=0, tiled=True)
+    sent = jnp.stack([d_share] * lax.axis_size("member"))
+    d_pre = jnp.concatenate(lax.all_to_all(sent, "member", 0, 0), axis=0)
     g_down = contract(d_in, act_full, 0, 0)
     g_up = contract(x_in, d_pre, 0, 1)
     dx_part = contract(d_pre, up_own, 0, 1)

time: 535 us -> 563 us (1.052)
  waiting for transfers between devices: 382 us -> 411 us
    all_to_all x0 -> x1, waiting for transfers between devices: none -> 44.9 us  [body(): d_pre = jnp.concatenate(lax.all_to_all(sent, 'member', 0, 0), axis=0)]
    all_gather x1 -> x0, waiting for transfers between devices: 37.1 us -> none  [body(): d_pre = lax.all_gather(d_share, 'member', axis=0, tiled=True)]
    all_to_all x1, waiting for transfers between devices: 0.01 us -> 21 us  [body(): lax.all_to_all(y_part.reshape(dp_count, CAP, features).astype(jnp.bfloat1...]
    all_to_all x1, starting transfers between devices: 13 us -> 4.05 us  [body(): lax.all_to_all(dx_part.reshape(dp_count, CAP, features).astype(jnp.bfloat...]
  transfers between devices with their start and end apart: 8 -> 8, of which waited for: 7 -> 8; matrix products, arithmetic and copies ran while one was open for 12% -> 12% of each run, Pallas kernels for 0% -> 0%
where the time goes in v1:
time: 563 us; the launch traced here: 562 us
  waiting for transfers between devices  411 us (73%)
  starting transfers between devices  53.2 us (9%)
  local copies, waits for them, and re-layouts  39.6 us (7%)
  matrix products  29.2 us (5%)
  between operations  14.9 us (3%)
  other arithmetic  13.5 us (2%)
    psum x1, waiting for transfers between devices, body(): pre_full = lax.psum(partial_value, 'member').astype(jnp.float32)  156 us
    all_to_all x1, waiting for transfers between devices, body(): lax.all_to_all(down_parts, 'dp', split_axis=0, concat_axis=1, tiled=True)  47.9 us
    all_to_all x1, waiting for transfers between devices, body(): d_pre = jnp.concatenate(lax.all_to_all(sent, 'member', 0, 0), axis=0)  44.9 us
    all_to_all x1, waiting for transfers between devices, body(): lax.all_to_all(spread(d_local), 'dp', split_axis=0, concat_axis=0, tiled=...  38 us
    all_to_all x1, waiting for transfers between devices, body(): lax.all_to_all(up_parts, 'dp', split_axis=0, concat_axis=1, tiled=True)  37.1 us
    all_to_all x1, waiting for transfers between devices, body(): lax.all_to_all(spread(x_local), 'dp', split_axis=0, concat_axis=0, tiled=...  36.7 us
    all_to_all x1, waiting for transfers between devices, body(): lax.all_to_all(dx_part.reshape(dp_count, CAP, features).astype(jnp.bfloat...  28.8 us
    dot_general x5, matrix products, contract(): lax.dot_general(left, right, (((left_dim,), (right_dim,)), ((), ())), pre...  22.6 us
  transfers between devices with their start and end apart: 8, of which 8 were waited for; matrix products, arithmetic and copies ran while one was open for 12% of the time, Pallas kernels for 0%

profile of v1, /device:TPU:1, one launch (start us, length us, event | category | flops | bytes accessed | tf_op | source)
XLA Modules:
  0.0 561.6 jit_solution(6029290193083917425)
XLA Ops:
  7.2 0.0 copy-start
  7.2 0.8 copy.37
  8.0 0.1 eq.44
  8.1 0.1 eq.40
  8.3 0.6 reduce-window.6
  8.9 0.2 slice_reduce_fusion
  9.1 0.1 fusion.14
  9.2 0.1 reshape.103
  9.4 0.1 copy.39
  9.4 0.7 multiply_add_fusion
  10.1 0.8 convert_reduce_fusion.2
  10.9 0.0 copy-done
  10.9 0.3 convolution_convert_fusion.6
  11.2 0.9 broadcast_in_dim.36
  12.1 16.8 %all-to-all-start.4 = ((bf16[32,34,256]{2,1,0:T(8,128)(2,1)}), bf16[32,34,256]{2,1,0:T(8,128)(2,1)S(1)}, u32[]{:S(2)}, u32[]{:S(2)}) async-start(bf16[32,34,256]{2,1,0:T(8,128)(2,1)} %bitcast.9), calls=%async_computation.4 | async-start | bytes 1310720 | tf_op jit(solution)/shard_map/all_to_all | solution.py:82
  28.9 1.0 convolution_convert_fusion.7
  30.0 38.0 %all-to-all-done.4 = bf16[32,34,256]{2,1,0:T(8,128)(2,1)S(1)} async-done(((bf16[32,34,256]{2,1,0:T(8,128)(2,1)}), bf16[32,34,256]{2,1,0:T(8,128)(2,1)S(1)}, u32[]{:S(2)}, u32[]{:S(2)}) %all-to-all-start.4) | async-done | bytes 557088 | tf_op jit(solution)/shard_map/all_to_all | solution.py:82
  68.0 0.9 broadcast_in_dim.34
  68.8 4.1 all-to-all-start
  72.9 1.3 fusion.16
  74.3 1.0 pad_maximum_fusion.1
  75.3 36.7 %all-to-all-done = bf16[32,34,256]{2,1,0:T(8,128)(2,1)S(1)} async-done(((bf16[32,34,256]{2,1,0:T(8,128)(2,1)}), bf16[32,34,256]{2,1,0:T(8,128)(2,1)S(1)}, u32[]{:S(2)}, u32[]{:S(2)}) %all-to-all-start) | async-done | bytes 557088 | tf_op jit(solution)/shard_map/all_to_all | solution.py:67
  112.0 0.0 copy-start.2
  112.0 0.8 copy-done.2
  112.8 4.5 all-to-all-start.2
  117.3 1.3 fusion.17
  118.6 1.0 pad_maximum_fusion
  119.7 47.9 %all-to-all-done.2 = bf16[32,8,1792]{2,1,0:T(8,128)(2,1)S(1)} async-done(((bf16[32,8,1792]{2,1,0:T(8,128)(2,1)}), bf16[32,8,1792]{2,1,0:T(8,128)(2,1)S(1)}, u32[]{:S(2)}, u32[]{:S(2)}) %all-to-all-start.2) | async-done | bytes 917536 | tf_op jit(solution)/shard_map/all_to_all | solution.py:38
  167.6 4.5 all-to-all-start.1
  172.1 0.0 all-reduce.4.cloned.1.call-start
  172.2 1.0 reshape.114
  173.1 1.3 reshape.105
  174.4 4.4 convolution_convert_fusion
  178.8 6.5 %copy.40 = bf16[1792,1088]{0,1:T(8,128)(2,1)} copy(bf16[1792,1088]{1,0:T(8,128)(2,1)} %convolution_convert_fusion) | data formatting | bytes 7798784 | tf_op jit(solution)/shard_map/convert_element_type | solution.py:86
  185.2 37.1 %all-to-all-done.1 = bf16[32,8,1792]{2,1,0:T(8,128)(2,1)S(1)} async-done(((bf16[32,8,1792]{2,1,0:T(8,128)(2,1)}), bf16[32,8,1792]{2,1,0:T(8,128)(2,1)S(1)}, u32[]{:S(2)}, u32[]{:S(2)}) %all-to-all-start.1) | async-done | bytes 917536 | tf_op jit(solution)/shard_map/all_to_all | solution.py:37
  222.4 3.1 convolution_convert_fusion.1
  225.5 0.0 all-reduce.4.cloned.1.call-update
  225.5 1.3 dynamic-slice
  227.4 156.5 %all-reduce.4.cloned.1.call-done = (bf16[1088,1792]{1,0:T(8,128)(2,1)}, bf16[1792,1088]{0,1:T(8,128)(2,1)}) async-done(((bf16[1088,1792]{1,0:T(8,128)(2,1)}, bf16[1792,1088]{0,1:T(8,128)(2,1)}), (bf16[1088,1792]{1,0:T(8,128)(2,1)}, bf16[1792,1088]{0,1:T(8,128)(2,1)})) %all-reduce.4.cloned.1.call-update) | async-done | bytes 7798800 | tf_op jit(solution)/shard_map/psum | solution.py:71
  383.9 2.7 convert_element_type.65
  386.6 1.4 fusion.11
  388.0 0.2 copy.41
  388.2 2.2 stack.2
  390.5 5.1 all-to-all-start.5
  395.6 5.1 multiply_convert_fusion
  400.7 6.9 %dot_general.38 = bf16[32,34,1792]{2,1,0:T(8,128)(2,1)} reshape(bf16[1088,1792]{1,0:T(8,128)(2,1)} %multiply_convert_fusion) | data formatting | bytes 7798784 | tf_op jit(solution)/shard_map/dot_general | solution.py:12
  407.6 4.6 convolution_convert_fusion.5
  412.2 44.9 %all-to-all-done.5 = bf16[16,112,1088]{2,1,0:T(8,128)(2,1)} async-done(((bf16[16,112,1088]{2,1,0:T(8,128)(2,1)}), bf16[16,112,1088]{2,1,0:T(8,128)(2,1)}, u32[]{:S(2)}, u32[]{:S(2)}) %all-to-all-start.5) | async-done | bytes 3899424 | tf_op jit(solution)/shard_map/all_to_all | solution.py:96
  457.0 14.2 %all-to-all-start.3 = ((bf16[32,34,256]{2,1,0:T(8,128)(2,1)}), bf16[32,34,256]{2,1,0:T(8,128)(2,1)S(1)}, u32[]{:S(2)}, u32[]{:S(2)}) async-start(bf16[32,34,256]{2,1,0:T(8,128)(2,1)} %convolution_convert_fusion.5), calls=%async_computation.3 | async-start | bytes 1310720 | tf_op jit(solution)/shard_map/all_to_all | solution.py:75
  471.2 6.4 %copy.42 = bf16[1088,1792]{1,0:T(8,128)(2,1)} copy(bf16[1088,1792]{0,1:T(8,128)(2,1)} %bitcast.12) | data formatting | bytes 7798784 | tf_op jit(solution)/shard_map/dot_general | solution.py:12
  477.6 6.9 %dot_general.44 = bf16[32,34,1792]{2,1,0:T(8,128)(2,1)} reshape(bf16[1088,1792]{1,0:T(8,128)(2,1)} %copy.42) | data formatting | bytes 7798784 | tf_op jit(solution)/shard_map/dot_general | solution.py:12
  484.6 0.0 copy-start.3
  484.6 4.7 convolution_convert_fusion.4
  489.3 21.0 %all-to-all-done.3 = bf16[32,34,256]{2,1,0:T(8,128)(2,1)S(1)} async-done(((bf16[32,34,256]{2,1,0:T(8,128)(2,1)}), bf16[32,34,256]{2,1,0:T(8,128)(2,1)S(1)}, u32[]{:S(2)}, u32[]{:S(2)}) %all-to-all-start.3) | async-done | bytes 557088 | tf_op jit(solution)/shard_map/all_to_all | solution.py:75
  510.3 4.1 all-to-all-start.6
  514.4 0.0 copy-done.3
  514.4 4.4 fusion.1
  518.8 0.1 convert_reduce_fusion.1
  518.9 1.1 convolution_convert_fusion.9
  520.1 4.5 fusion
  524.6 28.8 %all-to-all-done.6 = bf16[32,34,256]{2,1,0:T(8,128)(2,1)S(1)} async-done(((bf16[32,34,256]{2,1,0:T(8,128)(2,1)}), bf16[32,34,256]{2,1,0:T(8,128)(2,1)S(1)}, u32[]{:S(2)}, u32[]{:S(2)}) %all-to-all-start.6) | async-done | bytes 557088 | tf_op jit(solution)/shard_map/all_to_all | solution.py:101
  553.4 0.1 convert_reduce_fusion
  553.6 1.1 convolution_convert_fusion.8
  554.7 0.0 copy-done.1
  (8 shorter events, 0.2 us)
Async XLA Ops:
  7.2 3.7 copy-start
  12.1 55.9 %all-to-all-start.4 = ((bf16[32,34,256]{2,1,0:T(8,128)(2,1)}), bf16[32,34,256]{2,1,0:T(8,128)(2,1)S(1)}, u32[]{:S(2)}, u32[]{:S(2)}) async-start(bf16[32,34,256]{2,1,0:T(8,128)(2,1)} %bitcast.9), calls=%async_computation.4 | async-start | bytes 1310720 | tf_op jit(solution)/shard_map/all_to_all | solution.py:82
  68.8 43.1 %all-to-all-start = ((bf16[32,34,256]{2,1,0:T(8,128)(2,1)}), bf16[32,34,256]{2,1,0:T(8,128)(2,1)S(1)}, u32[]{:S(2)}, u32[]{:S(2)}) async-start(bf16[32,34,256]{2,1,0:T(8,128)(2,1)} %bitcast.2), calls=%async_computation | async-start | bytes 1310720 | tf_op jit(solution)/shard_map/all_to_all | solution.py:67
  112.0 0.8 copy-start.2
  112.8 54.7 %all-to-all-start.2 = ((bf16[32,8,1792]{2,1,0:T(8,128)(2,1)}), bf16[32,8,1792]{2,1,0:T(8,128)(2,1)S(1)}, u32[]{:S(2)}, u32[]{:S(2)}) async-start(bf16[32,8,1792]{2,1,0:T(8,128)(2,1)} %bitcast.5), calls=%async_computation.2 | async-start | bytes 1835008 | tf_op jit(solution)/shard_map/all_to_all | solution.py:38
  167.6 54.8 %all-to-all-start.1 = ((bf16[32,8,1792]{2,1,0:T(8,128)(2,1)}), bf16[32,8,1792]{2,1,0:T(8,128)(2,1)S(1)}, u32[]{:S(2)}, u32[]{:S(2)}) async-start(bf16[32,8,1792]{2,1,0:T(8,128)(2,1)} %bitcast.3), calls=%async_computation.1 | async-start | bytes 1835008 | tf_op jit(solution)/shard_map/all_to_all | solution.py:37
  172.1 211.8 %all-reduce.4.cloned.1.call-start = ((), (), s32[]{:S(2)}) async-start(), calls=%async_computation.7 | async-start | bytes 15597568 | tf_op jit(solution)/shard_map/psum | solution.py:71
  390.5 66.6 %all-to-all-start.5 = ((bf16[16,112,1088]{2,1,0:T(8,128)(2,1)}), bf16[16,112,1088]{2,1,0:T(8,128)(2,1)}, u32[]{:S(2)}, u32[]{:S(2)}) async-start(bf16[16,112,1088]{2,1,0:T(8,128)(2,1)} %stack.2), calls=%async_computation.5 | async-start | bytes 8257536 | tf_op jit(solution)/shard_map/all_to_all | solution.py:96
  457.0 53.3 %all-to-all-start.3 = ((bf16[32,34,256]{2,1,0:T(8,128)(2,1)}), bf16[32,34,256]{2,1,0:T(8,128)(2,1)S(1)}, u32[]{:S(2)}, u32[]{:S(2)}) async-start(bf16[32,34,256]{2,1,0:T(8,128)(2,1)} %convolution_convert_fusion.5), calls=%async_computation.3 | async-start | bytes 1310720 | tf_op jit(solution)/shard_map/all_to_all | solution.py:75
  484.6 29.8 %copy-start.3 = (bf16[1088,256]{1,0:T(8,128)(2,1)S(1)}, bf16[1088,256]{1,0:T(8,128)(2,1)}, u32[]{:S(2)}) copy-start(bf16[1088,256]{1,0:T(8,128)(2,1)} %reshape.114) | copy-start | bytes 1671172
  510.3 43.1 %all-to-all-start.6 = ((bf16[32,34,256]{2,1,0:T(8,128)(2,1)}), bf16[32,34,256]{2,1,0:T(8,128)(2,1)S(1)}, u32[]{:S(2)}, u32[]{:S(2)}) async-start(bf16[32,34,256]{2,1,0:T(8,128)(2,1)} %convolution_convert_fusion.4), calls=%async_computation.6 | async-start | bytes 1310720 | tf_op jit(solution)/shard_map/all_to_all | solution.py:101
  520.1 34.7 %copy-start.1 = (bf16[128,256]{1,0:T(8,128)(2,1)S(1)}, bf16[128,256]{1,0:T(8,128)(2,1)}, u32[]{:S(2)}) copy-start(bf16[128,256]{1,0:T(8,128)(2,1)} %param.11) | copy-start | bytes 196612
Sparse Core Ops, SparseCore 0:
  225.6 158.2 all-reduce.3
